TPU v7x, 32 devices: a whole 2x2x4 slice. The times are simulated.
32 devices in a mesh: slide: 2 (over y), tile: 16 (over z, x, core).
Axes of the slice: x: 2, y: 2, z: 4, core: 2. Of those that a mesh axis runs over, the one named last changes fastest.
Arguments:
- fine_level: bfloat16 [2, 128, 256, 256], P('slide', 'tile'), may hold values from -6 to 6
- coarse_level: bfloat16 [2, 64, 128, 256], P('slide', 'tile'), may hold values from -6 to 6
- fine_kernel: bfloat16 [256, 9, 128], replicated, may hold values from -0.125 to 0.125
- coarse_kernel: bfloat16 [256, 9, 128], replicated, may hold values from -0.125 to 0.125
- fine_gain: float32 [128], replicated, may hold values from 0.25 to 1.75
- fine_offset: float32 [128], replicated, may hold values from -3 to 3
- coarse_gain: float32 [128], replicated, may hold values from 0.25 to 1.75
- coarse_offset: float32 [128], replicated, may hold values from -3 to 3
- class_kernel: bfloat16 [8, 128], replicated
- class_offset: float32 [8], replicated, may hold values from -4 to 4
- tissue_labels: int32 [2, 128, 256], P('slide', 'tile'), may hold values from -1 to 7, as said below
Outputs:
- loss: float32 [], replicated
- head_grads: float32 [12, 128], replicated
- conv_grads: float32 [256, 2, 9, 128], P('tile')
Inputs may be any that keep to these rules, and one draw needn't show every extreme that they name: `tissue_labels`: -1 marks a pixel without tissue, other values are classes.
All inputs are finite; a program needn't handle non-finite values.
Results may differ from a plain program's by a relative error of at most 0.0033.
Values may be sent and summed in bfloat16 or wider, within the bound.
A program may use at most 128 MiB of HBM per device.

v0:
```python
import jax
import jax.numpy as jnp
from jax import lax
from jax.sharding import PartitionSpec as P

GROUPS = 32
epsilon = 1e-05


def padded_2(cells, sides, width):
    for axis, dim in sides:
        count = lax.axis_size(axis)
        ends = count - 1
        head = lax.slice_in_dim(cells, 0, width, axis=dim)
        tail = lax.slice_in_dim(cells, cells.shape[dim] - width, cells.shape[dim], axis=dim)
        cells = jnp.concatenate(
            [
                lax.ppermute(tail, axis, [(i, (i + 1) % count) for i in range(ends)]),
                cells,
                lax.ppermute(head, axis, [((i + 1) % count, i) for i in range(ends)]),
            ],
            axis=dim,
        )
    return cells


def shifted(padded, height, width, position):
    row_step = position // 3
    col_step = position % 3
    return padded[row_step : row_step + height, col_step : col_step + width].reshape(
        height * width, -1
    )


def convolve(padded, kernel, height, width):
    total = jnp.zeros((height * width, kernel.shape[2]), jnp.float32)
    for position in range(9):
        total = total + jnp.dot(
            shifted(padded, height, width, position),
            kernel[:, position, :],
            preferred_element_type=jnp.float32,
        )
    return total


def group_sums(values, groups):
    return values.reshape(values.shape[0], groups, -1).sum(axis=(0, 2))


def spread(per_group, channels):
    return jnp.repeat(per_group, channels // per_group.shape[0])


def per_device(
    fine_level,
    coarse_level,
    fine_kernel,
    coarse_kernel,
    fine_gain,
    fine_offset,
    coarse_gain,
    coarse_offset,
    class_kernel,
    class_offset,
    tissue_labels,
):
    tiles = lax.axis_size("tile")
    channels = fine_kernel.shape[2]
    in_channels = fine_kernel.shape[0]
    height, width = (fine_level.shape[1], fine_level.shape[2])
    labels = tissue_labels[0].reshape(-1)
    tissue = (labels >= 0).astype(jnp.float32)
    total = lax.psum(jnp.sum(tissue), ("slide", "tile"))
    fine_rows = padded_2(fine_level[0], (("tile", 0),), 1)
    coarse_rows = padded_2(coarse_level[0], (("tile", 0),), 1)
    fine_pad = jnp.pad(fine_rows, ((0, 0), (1, 1), (0, 0)))
    coarse_pad = jnp.pad(coarse_rows, ((0, 0), (1, 1), (0, 0)))
    fine_conv = convolve(fine_pad, fine_kernel, height, width)
    coarse_conv = convolve(coarse_pad, coarse_kernel, height // 2, width // 2)
    stats = lax.psum(
        (
            group_sums(fine_conv, GROUPS),
            group_sums(fine_conv * fine_conv, GROUPS),
            group_sums(coarse_conv, GROUPS),
            group_sums(coarse_conv * coarse_conv, GROUPS),
        ),
        "tile",
    )
    fine_number = height * tiles * width * (channels // GROUPS)
    coarse_number = fine_number // 4

    def normalize(conv_out, first_sum, square_sum, number, gain, offset):
        mean = first_sum / number
        variance = square_sum / number - mean * mean
        scale = spread(lax.rsqrt(variance + epsilon), channels)
        normed = (conv_out - spread(mean, channels)) * scale
        return (normed, scale, normed * gain + offset)

    fine_normed, fine_scale, fine_pre = normalize(
        fine_conv, stats[0], stats[1], fine_number, fine_gain, fine_offset
    )
    coarse_normed, coarse_scale, coarse_pre = normalize(
        coarse_conv, stats[2], stats[3], coarse_number, coarse_gain, coarse_offset
    )
    act_coarse = jnp.maximum(coarse_pre, 0.0).reshape(height // 2, width // 2, channels)
    upsampled = jnp.repeat(jnp.repeat(act_coarse, 2, 0), 2, 1).reshape(height * width, channels)
    merged = (jnp.maximum(fine_pre, 0.0) + upsampled).astype(jnp.bfloat16)
    logits = (
        lax.dot_general(
            class_kernel, merged, (((1,), (1,)), ((), ())), preferred_element_type=jnp.float32
        )
        + class_offset[:, None]
    )
    onehot = (
        labels[None, :] == jnp.arange(class_kernel.shape[0], dtype=jnp.int32)[:, None]
    ).astype(jnp.float32)
    top = jnp.max(logits, axis=0)
    lse = top + jnp.log(jnp.sum(jnp.exp(logits - top[None, :]), axis=0))
    loss_local = jnp.sum((lse - jnp.sum(onehot * logits, axis=0)) * tissue)
    dlogits = ((jnp.exp(logits - lse[None, :]) - onehot) * tissue[None, :] / total).astype(
        jnp.bfloat16
    )
    class_grad = jnp.dot(dlogits, merged, preferred_element_type=jnp.float32)
    dmerged = lax.dot_general(
        dlogits, class_kernel, (((0,), (0,)), ((), ())), preferred_element_type=jnp.float32
    )
    dact_coarse = (
        dmerged.reshape(height // 2, 2, width // 2, 2, channels)
        .sum(axis=(1, 3))
        .reshape(-1, channels)
    )
    fine_dpre = dmerged * (fine_pre > 0).astype(jnp.float32)
    coarse_dpre = dact_coarse * (coarse_pre > 0).astype(jnp.float32)
    fine_dnorm = fine_dpre * fine_gain
    coarse_dnorm = coarse_dpre * coarse_gain
    back = lax.psum(
        (
            group_sums(fine_dnorm, GROUPS),
            group_sums(fine_dnorm * fine_normed, GROUPS),
            group_sums(coarse_dnorm, GROUPS),
            group_sums(coarse_dnorm * coarse_normed, GROUPS),
        ),
        "tile",
    )
    fine_dconv = (
        (
            fine_dnorm
            - spread(back[0] / fine_number, channels)
            - fine_normed * spread(back[1] / fine_number, channels)
        )
        * fine_scale
    ).astype(jnp.bfloat16)
    coarse_dconv = (
        (
            coarse_dnorm
            - spread(back[2] / coarse_number, channels)
            - coarse_normed * spread(back[3] / coarse_number, channels)
        )
        * coarse_scale
    ).astype(jnp.bfloat16)
    head_local = jnp.concatenate(
        [
            jnp.stack(
                [
                    jnp.sum(fine_dpre * fine_normed, axis=0),
                    jnp.sum(fine_dpre, axis=0),
                    jnp.sum(coarse_dpre * coarse_normed, axis=0),
                    jnp.sum(coarse_dpre, axis=0),
                ],
                0,
            ),
            class_grad,
        ],
        0,
    )
    head_grads, loss_total = lax.psum((head_local, loss_local), ("slide", "tile"))
    sections = []
    for padded, upstream, rows_here, cols_here in (
        (fine_pad, fine_dconv, height, width),
        (coarse_pad, coarse_dconv, height // 2, width // 2),
    ):
        stacked = jnp.concatenate(
            [shifted(padded, rows_here, cols_here, position) for position in range(9)], 1
        )
        product = lax.dot_general(
            stacked, upstream, (((0,), (0,)), ((), ())), preferred_element_type=jnp.float32
        )
        sections.append(product.reshape(9, in_channels, channels).transpose(1, 0, 2))
    whole = lax.psum(jnp.stack(sections, 1), "slide")
    conv_grads = lax.psum_scatter(whole, "tile", scatter_dimension=0, tiled=True)
    return (loss_total / total, head_grads, conv_grads)


def solution(mesh):
    return jax.shard_map(
        per_device,
        mesh=mesh,
        in_specs=(
            P("slide", "tile", None, None),
            P("slide", "tile", None, None),
            P(),
            P(),
            P(),
            P(),
            P(),
            P(),
            P(),
            P(),
            P("slide", "tile", None),
        ),
        out_specs=(P(), P(), P("tile", None, None, None)),
        check_vma=False,
    )
```

profile of v0, /device:TPU:0, one launch (start us, length us, event | category | flops | bytes accessed | tf_op | source)
XLA Modules:
  0.0 292.0 jit_solution(8008616227894665407)
XLA Ops:
  8.1 2.4 collective-permute-start.2
  10.5 1.3 collective-permute-start.3
  12.8 5.3 %collective-permute-start = (bf16[1,256,256]{2,1,0:T(8,128)(2,1)S(1)}, bf16[1,256,256]{2,1,0:T(8,128)(2,1)S(1)}, u32[]{:S(2)}, u32[]{:S(2)}) collective-permute-start(bf16[1,256,256]{2,1,0:T(8,128)(2,1)S(1)} %get-tuple-element.43), channel_id=1, source_target_pairs={{0,1},{1,2},{2,3},{3,4},{4,5},{5,6},{6,7},{7,8},{8,9},{9,10},{10,1... | collective-permute-start | bytes 393224 | tf_op jit(solution)/shard_map/ppermute | solution.py:18
  18.1 1.3 collective-permute-start.1
  34.2 1.3 constant_dynamic-update-slice_fusion.8
  39.5 1.6 fusion.80
  41.6 34.9 %all-reduce.4 = (f32[32]{0:T(128)S(1)}, f32[32]{0:T(128)S(1)}, f32[32]{0:T(128)S(1)}, f32[32]{0:T(128)S(1)}) all-reduce(f32[32]{0:T(128)S(1)} %copy-done.30, f32[32]{0:T(128)S(1)} %copy-done.29, f32[32]{0:T(128)S(1)} %reduce_sum.178, f32[32]{0:T(128)S(1)} %reduce_sum.175), channel_id=1, replica_groups=mesh['slide'=2,'tile'=16] {'tile'}, use_global_device_ids=true, to_apply=%region_11.12 | all-reduce | flops 128 | bytes 1024 | tf_op jit(solution)/shard_map/psum | solution.py:80
  80.5 37.0 %psum.89 = f32[]{:T(128)} all-reduce(f32[]{:T(128)} %get-tuple-element.20), channel_id=1, replica_groups=mesh['slide'=2,'tile'=16] {'slide','tile'}, use_global_device_ids=true, to_apply=%region_18.19 | all-reduce | flops 1 | bytes 8 | tf_op jit(solution)/shard_map/psum | solution.py:73
  117.5 4.0 %multiply_reduce_fusion.3 = (f32[128]{0:T(128)S(1)}, f32[128]{0:T(128)}, f32[128]{0:T(128)}, f32[128]{0:T(128)S(1)}, f32[2048,128]{1,0:T(8,128)}) fusion(f32[128]{0:T(128)} %param.15, f32[128]{0:T(128)} %param.16, f32[128]{0:T(128)} %copy-done.25, f32[2048,128]{1,0:T(8,128)} %get-tuple-element.60, f32[128]{0:T(128)} %copy-done.27, ...), kind=kOutput, calls=%fused_computation.38 | convolution fusion | flops 7716352 | bytes 2193412 | tf_op jit(solution)/shard_map/dot_general | solution.py:124
  122.0 2.7 reduce_sum.227
  124.7 1.8 multiply_reduce_fusion.4
  126.9 32.5 %all-reduce.3 = (f32[32]{0:T(128)S(1)}, f32[32]{0:T(128)S(1)}, f32[32]{0:T(128)S(1)}, f32[32]{0:T(128)S(1)}) all-reduce(f32[32]{0:T(128)S(1)} %reduce_sum.241, f32[32]{0:T(128)S(1)} %reduce_sum.238, f32[32]{0:T(128)S(1)} %reduce_sum.235, f32[32]{0:T(128)S(1)} %reduce_sum.232), channel_id=1, replica_groups=mesh['slide'=2,'tile'=16] {'tile'}, use_global_device_ids=true, to_apply=%region_36.37 | all-reduce | flops 128 | bytes 1024 | tf_op jit(solution)/shard_map/psum | solution.py:136
  160.2 2.5 constant_dynamic-update-slice_fusion.7
  163.8 1.1 constant_dynamic-update-slice_fusion.5
  164.9 1.1 constant_dynamic-update-slice_fusion.4
  167.1 1.2 constant_dynamic-update-slice_fusion.2
  168.4 1.1 constant_dynamic-update-slice_fusion.1
  169.5 1.2 constant_dynamic-update-slice_fusion
  170.7 5.4 %fusion.9 = f32[2304,128]{1,0:T(8,128)S(1)} fusion(bf16[2048,2304]{1,0:T(8,128)(2,1)} %constant_dynamic-update-slice_fusion, f32[2048,128]{1,0:T(8,128)S(1)} %copy-done.15, f32[128]{0:T(128)S(1)} %mul.148, f32[128]{0:T(128)S(1)} %sub.99, f32[128]{0:T(128)S(1)} %copy-done.35, f32[128]{0:T(128)S(1)} %copy-done.26, f32[128]{0:T(128)S(1)} %copy-done.28, ...), kind=kOutput, calls=%fused_computation.40 | convolution fusion | flops 1211105280 | bytes 12717056 | tf_op jit(solution)/shard_map/dot_general | solution.py:185
  176.1 2.5 fusion.21
  178.6 1.6 pad_maximum_fusion
  180.3 59.6 %reduce-scatter.2.cloned.1.call-done = f32[16,2,9,128]{3,0,2,1:T(8,128)} async-done(((f32[256,2,9,128]{3,0,2,1:T(8,128)}), f32[16,2,9,128]{3,0,2,1:T(8,128)}) %reduce-scatter.2.cloned.1.call-update) | async-done | bytes 147472 | tf_op jit(solution)/shard_map/reduce_scatter | solution.py:190
  240.9 40.0 %all-reduce.2 = (f32[]{:T(128)}, f32[12,128]{1,0:T(8,128)}) all-reduce(f32[]{:T(128)} %get-tuple-element.21, f32[12,128]{1,0:T(8,128)S(1)} %concatenate.33), channel_id=1, replica_groups=mesh['slide'=2,'tile'=16] {'slide','tile'}, use_global_device_ids=true, to_apply=%region_16.17 | all-reduce | flops 1537 | bytes 12296 | tf_op jit(solution)/shard_map/psum | solution.py:176
  282.3 1.6 copy.16
  (173 shorter events, 29.6 us)
Async XLA Ops:
  7.2 72.4 %copy-start = (bf16[8,128]{1,0:T(8,128)(2,1)S(1)}, bf16[8,128]{1,0:T(8,128)(2,1)}, u32[]{:S(2)}) copy-start(bf16[8,128]{1,0:T(8,128)(2,1)} %param.19) | copy-start | bytes 6148
  7.2 232.8 %reduce-scatter.2.cloned.1.call-start = ((), (), s32[]{:S(2)}) async-start(), calls=%async_computation.1 | async-start | bytes 2506752 | tf_op jit(solution)/shard_map/reduce_scatter | solution.py:190
  8.1 12.6 %collective-permute-start.2 = (bf16[1,128,256]{2,1,0:T(8,128)(2,1)S(1)}, bf16[1,128,256]{2,1,0:T(8,128)(2,1)S(1)}, u32[]{:S(2)}, u32[]{:S(2)}) collective-permute-start(bf16[1,128,256]{2,1,0:T(8,128)(2,1)S(1)} %get-tuple-element.53), channel_id=1, source_target_pairs={{0,1},{1,2},{2,3},{3,4},{4,5},{5,6},{6,7},{7,8},{8,9},{9,10},{10,1... | collective-permute-start | bytes 196616 | tf_op jit(solution)/shard_map/ppermute | solution.py:18
  10.5 10.2 %collective-permute-start.3 = (bf16[1,128,256]{2,1,0:T(8,128)(2,1)S(1)}, bf16[1,128,256]{2,1,0:T(8,128)(2,1)S(1)}, u32[]{:S(2)}, u32[]{:S(2)}) collective-permute-start(bf16[1,128,256]{2,1,0:T(8,128)(2,1)S(1)} %get-tuple-element.54), channel_id=1, source_target_pairs={{1,0},{2,1},{3,2},{4,3},{5,4},{6,5},{7,6},{8,7},{9,8},{10,9},{11,1... | collective-permute-start | bytes 196616 | tf_op jit(solution)/shard_map/ppermute | solution.py:20
  12.8 9.9 %copy-start.19 = (bf16[256,9,128]{2,0,1:T(8,128)(2,1)S(1)}, bf16[256,9,128]{2,0,1:T(8,128)(2,1)}, u32[]{:S(2)}) copy-start(bf16[256,9,128]{2,0,1:T(8,128)(2,1)} %param.14) | copy-start | bytes 1769476
  12.8 19.7 %collective-permute-start = (bf16[1,256,256]{2,1,0:T(8,128)(2,1)S(1)}, bf16[1,256,256]{2,1,0:T(8,128)(2,1)S(1)}, u32[]{:S(2)}, u32[]{:S(2)}) collective-permute-start(bf16[1,256,256]{2,1,0:T(8,128)(2,1)S(1)} %get-tuple-element.43), channel_id=1, source_target_pairs={{0,1},{1,2},{2,3},{3,4},{4,5},{5,6},{6,7},{7,8},{8,9},{9,10},{10,1... | collective-permute-start | bytes 393224 | tf_op jit(solution)/shard_map/ppermute | solution.py:18
  18.1 14.4 %collective-permute-start.1 = (bf16[1,256,256]{2,1,0:T(8,128)(2,1)S(1)}, bf16[1,256,256]{2,1,0:T(8,128)(2,1)S(1)}, u32[]{:S(2)}, u32[]{:S(2)}) collective-permute-start(bf16[1,256,256]{2,1,0:T(8,128)(2,1)S(1)} %get-tuple-element.44), channel_id=1, source_target_pairs={{1,0},{2,1},{3,2},{4,3},{5,4},{6,5},{7,6},{8,7},{9,8},{10,9},{11,1... | collective-permute-start | bytes 393224 | tf_op jit(solution)/shard_map/ppermute | solution.py:20
  27.2 5.9 %copy-start.1 = (bf16[1,8,256,256]{3,2,1,0:T(8,128)(2,1)S(1)}, bf16[1,8,256,256]{3,2,1,0:T(8,128)(2,1)}, u32[]{:S(2)}) copy-start(bf16[1,8,256,256]{3,2,1,0:T(8,128)(2,1)} %param.11) | copy-start | bytes 3145732
  34.2 2.9 %copy-start.4 = (bf16[8,256,256]{2,1,0:T(8,128)(2,1)}, bf16[8,256,256]{2,1,0:T(8,128)(2,1)S(1)}, u32[]{:S(2)}) copy-start(bf16[8,256,256]{2,1,0:T(8,128)(2,1)S(1)} %get-tuple-element.38) | copy-start | bytes 3145732
  34.2 3.5 %copy-start.2 = (bf16[8,256,256]{2,1,0:T(8,128)(2,1)}, bf16[8,256,256]{2,1,0:T(8,128)(2,1)S(1)}, u32[]{:S(2)}) copy-start(bf16[8,256,256]{2,1,0:T(8,128)(2,1)S(1)} %get-tuple-element.37) | copy-start | bytes 3145732
  36.7 2.8 copy-start.8
  39.5 37.7 %copy-start.24 = (f32[128]{0:T(128)S(1)}, f32[128]{0:T(128)}, u32[]{:S(2)}) copy-start(f32[128]{0:T(128)} %param.17) | copy-start | bytes 1540
  39.5 37.7 %copy-start.31 = (f32[128]{0:T(128)S(1)}, f32[128]{0:T(128)}, u32[]{:S(2)}) copy-start(f32[128]{0:T(128)} %param.18) | copy-start | bytes 1540
  41.1 36.7 %copy-start.32 = (f32[128]{0:T(128)S(1)}, f32[128]{0:T(128)}, u32[]{:S(2)}) copy-start(f32[128]{0:T(128)} %param.16) | copy-start | bytes 1540
  41.1 36.7 %copy-start.34 = (f32[128]{0:T(128)S(1)}, f32[128]{0:T(128)}, u32[]{:S(2)}) copy-start(f32[128]{0:T(128)} %param.15) | copy-start | bytes 1540
  77.4 2.5 copy-start.23
  77.4 40.1 %copy-start.22 = (f32[2048]{0:T(1024)S(1)}, f32[2048]{0:T(1024)}, u32[]{:S(2)}) copy-start(f32[2048]{0:T(1024)} %compare_convert_fusion) | copy-start | bytes 24580
  160.2 2.5 copy-start.5
  160.2 3.6 %copy-start.3 = (bf16[8,256,256]{2,1,0:T(8,128)(2,1)S(1)}, bf16[8,256,256]{2,1,0:T(8,128)(2,1)}, u32[]{:S(2)}) copy-start(bf16[8,256,256]{2,1,0:T(8,128)(2,1)} %copy-done.2) | copy-start | bytes 3145732
  170.7 5.4 %copy-start.16 = (f32[512,128]{1,0:T(8,128)S(1)}, f32[512,128]{1,0:T(8,128)}, u32[]{:S(2)}) copy-start(f32[512,128]{1,0:T(8,128)} %get-tuple-element.32) | copy-start | bytes 786436
  180.2 59.7 %copy-start.13 = (bf16[2048,128]{1,0:T(8,128)(2,1)S(1)}, bf16[2048,128]{1,0:T(8,128)(2,1)}, u32[]{:S(2)}) copy-start(bf16[2048,128]{1,0:T(8,128)(2,1)} %copy-done.12) | copy-start | bytes 1572868
  180.3 60.6 %copy-start.36 = (f32[128]{0:T(128)S(1)}, f32[128]{0:T(128)}, u32[]{:S(2)}) copy-start(f32[128]{0:T(128)} %get-tuple-element.7) | copy-start | bytes 1540
  180.3 60.6 %copy-start.37 = (f32[128]{0:T(128)S(1)}, f32[128]{0:T(128)}, u32[]{:S(2)}) copy-start(f32[128]{0:T(128)} %get-tuple-element.8) | copy-start | bytes 1540
  180.3 102.1 %all-reduce.7.cloned.1.call-start = ((), (), s32[]{:S(2)}) async-start(), calls=%async_computation.2 | async-start | bytes 294912 | tf_op jit(solution)/shard_map/psum | solution.py:189
  (21 other events, 38.6 us)
Sparse Core Ops, SparseCore 0:
  180.4 59.5 reduce-scatter.1
  242.2 20.6 all-reduce.6
where the time goes:
time: 293 us; the launch traced here: 292 us
  blocking collectives  144 us (49%)
  waiting for transfers between devices  59.7 us (20%)
  local copies, waits for them, and re-layouts  28.9 us (10%)
  matrix products  20 us (7%)
  between operations  17.3 us (6%)
  other arithmetic  11.3 us (4%)
  starting transfers between devices  10.3 us (4%)
    reduce_scatter x1, waiting for transfers between devices, per_device(): lax.psum_scatter(whole, 'tile', scatter_dimension=0, tiled=True)  59.6 us
    psum x1, blocking collectives, per_device(): lax.psum((head_local, loss_local), ('slide', 'tile'))  40 us
    psum x1, blocking collectives, per_device(): total = lax.psum(jnp.sum(tissue), ('slide', 'tile'))  37 us
    psum x1, blocking collectives, per_device(): lax.psum((group_sums(fine_conv, GROUPS), group_sums(fine_conv * fine_conv...  34.9 us
    psum x1, blocking collectives, per_device(): lax.psum((group_sums(fine_dnorm, GROUPS), group_sums(fine_dnorm * fine_no...  32.5 us
    unnamed x96, local copies, waits for them, and re-layouts  21.5 us
    dot_general x2, matrix products, per_device(): lax.dot_general(stacked, upstream, (((0,), (0,)), ((), ())), preferred_el...  7.89 us
    ppermute x2, starting transfers between devices, padded_2(): lax.ppermute(tail, axis, [(i, (i + 1) % count) for i in range(ends)])  7.66 us
  transfers between devices with their start and end apart: 6, of which 1 were waited for; matrix products, arithmetic and copies ran while one was open for 5% of the time, Pallas kernels for 0%

commit v1 on v0

--- a/solution.py
+++ b/solution.py
@@ -173,7 +173,7 @@
         ],
         0,
     )
-    head_grads, loss_total = lax.psum((head_local, loss_local), ("slide", "tile"))
+    head_grads, loss_total = lax.psum(lax.psum((head_local, loss_local), "tile"), "slide")
     sections = []
     for padded, upstream, rows_here, cols_here in (
         (fine_pad, fine_dconv, height, width),

time: 293 us -> 303 us (1.034)
  waiting for transfers between devices: 59.7 us -> 75.5 us
  blocking collectives: 144 us -> 138 us
    psum x1, waiting for transfers between devices: 0.02 us -> 15.9 us  [per_device(): whole = lax.psum(jnp.stack(sections, 1), 'slide')]
    psum x2, blocking collectives: 72.6 us -> 66.2 us  [the longest x1 60.4 us: per_device(): lax.psum((head_local, loss_local), 'tile')]
  transfers between devices with their start and end apart: 6 -> 6, of which waited for: 1 -> 2; matrix products, arithmetic and copies ran while one was open for 5% -> 5% of each run, Pallas kernels for 0% -> 0%
where the time goes in v1:
time: 303 us; the launch traced here: 302 us
  blocking collectives  138 us (46%)
  waiting for transfers between devices  75.5 us (25%)
  local copies, waits for them, and re-layouts  29 us (10%)
  matrix products  20.5 us (7%)
  between operations  17.3 us (6%)
  other arithmetic  11.3 us (4%)
  starting transfers between devices  10.3 us (3%)
    psum x1, blocking collectives, per_device(): lax.psum((head_local, loss_local), 'tile')  60.4 us
    reduce_scatter x1, waiting for transfers between devices, per_device(): lax.psum_scatter(whole, 'tile', scatter_dimension=0, tiled=True)  59.6 us
    psum x1, blocking collectives, per_device(): total = lax.psum(jnp.sum(tissue), ('slide', 'tile'))  37 us
    psum x1, blocking collectives, per_device(): lax.psum((group_sums(fine_conv, GROUPS), group_sums(fine_conv * fine_conv...  34.9 us
    unnamed x96, local copies, waits for them, and re-layouts  21.6 us
    psum x1, waiting for transfers between devices, per_device(): whole = lax.psum(jnp.stack(sections, 1), 'slide')  15.9 us
    dot_general x2, matrix products, per_device(): lax.dot_general(stacked, upstream, (((0,), (0,)), ((), ())), preferred_el...  7.89 us
    ppermute x2, starting transfers between devices, padded_2(): lax.ppermute(tail, axis, [(i, (i + 1) % count) for i in range(ends)])  7.66 us
  transfers between devices with their start and end apart: 6, of which 2 were waited for; matrix products, arithmetic and copies ran while one was open for 5% of the time, Pallas kernels for 0%

profile of v1, /device:TPU:0, one launch (start us, length us, event | category | flops | bytes accessed | tf_op | source)
XLA Modules:
  0.0 302.0 jit_solution(8447467888476895846)
XLA Ops:
  8.1 2.4 collective-permute-start.2
  10.5 1.3 collective-permute-start.3
  12.8 5.3 %collective-permute-start = (bf16[1,256,256]{2,1,0:T(8,128)(2,1)S(1)}, bf16[1,256,256]{2,1,0:T(8,128)(2,1)S(1)}, u32[]{:S(2)}, u32[]{:S(2)}) collective-permute-start(bf16[1,256,256]{2,1,0:T(8,128)(2,1)S(1)} %get-tuple-element.45), channel_id=1, source_target_pairs={{0,1},{1,2},{2,3},{3,4},{4,5},{5,6},{6,7},{7,8},{8,9},{9,10},{10,1... | collective-permute-start | bytes 393224 | tf_op jit(solution)/shard_map/ppermute | solution.py:18
  18.1 1.3 collective-permute-start.1
  38.4 1.6 fusion.80
  40.5 34.9 %all-reduce.3 = (f32[32]{0:T(128)S(1)}, f32[32]{0:T(128)S(1)}, f32[32]{0:T(128)S(1)}, f32[32]{0:T(128)S(1)}) all-reduce(f32[32]{0:T(128)S(1)} %copy-done.31, f32[32]{0:T(128)S(1)} %copy-done.30, f32[32]{0:T(128)S(1)} %reduce_sum.178, f32[32]{0:T(128)S(1)} %reduce_sum.175), channel_id=1, replica_groups=mesh['slide'=2,'tile'=16] {'tile'}, use_global_device_ids=true, to_apply=%region_11.12 | all-reduce | flops 128 | bytes 1024 | tf_op jit(solution)/shard_map/psum | solution.py:80
  79.4 37.0 %psum.104 = f32[]{:T(128)} all-reduce(f32[]{:T(128)} %get-tuple-element.20), channel_id=1, replica_groups=mesh['slide'=2,'tile'=16] {'slide','tile'}, use_global_device_ids=true, to_apply=%region_19.20 | all-reduce | flops 1 | bytes 8 | tf_op jit(solution)/shard_map/psum | solution.py:73
  116.4 2.0 fusion.75
  118.4 3.4 %multiply_reduce_fusion.3 = (f32[128]{0:T(128)S(1)}, f32[128]{0:T(128)S(1)}, f32[128]{0:T(128)S(1)}, f32[128]{0:T(128)S(1)}, f32[2048,128]{1,0:T(8,128)}) fusion(f32[128]{0:T(128)} %param.15, f32[128]{0:T(128)} %param.16, f32[128]{0:T(128)} %copy-done.26, f32[2048,128]{1,0:T(8,128)} %get-tuple-element.62, f32[128]{0:T(128)} %copy-done.28, ...), kind=kOutput, calls=%fused_computation.38 | convolution fusion | flops 7716352 | bytes 2193412 | tf_op jit(solution)/shard_map/dot_general | solution.py:124
  121.8 1.2 constant_dynamic-update-slice_fusion.8
  123.4 2.7 reduce_sum.227
  126.2 1.8 multiply_reduce_fusion.4
  128.5 60.4 %all-reduce.2 = (f32[]{:T(128)}, f32[12,128]{1,0:T(8,128)S(1)}, f32[32]{0:T(128)S(1)}, f32[32]{0:T(128)S(1)}, f32[32]{0:T(128)S(1)}, /*index=5*/f32[32]{0:T(128)S(1)}) all-reduce(f32[]{:T(128)} %get-tuple-element.21, f32[12,128]{1,0:T(8,128)S(1)} %concatenate.33, ...), channel_id=1, replica_groups=mesh['slide'=2,'tile'=16] {'tile'}, use_global_device_ids=true, to_apply=%region_16.17 | all-reduce | flops 1665 | bytes 13320 | tf_op jit(solution)/shard_map/psum | solution.py:176
  189.6 2.5 constant_dynamic-update-slice_fusion.7
  196.5 1.2 constant_dynamic-update-slice_fusion.2
  197.8 1.1 constant_dynamic-update-slice_fusion.1
  198.9 1.2 constant_dynamic-update-slice_fusion
  200.1 5.4 %fusion.9 = f32[2304,128]{1,0:T(8,128)S(1)} fusion(bf16[2048,2304]{1,0:T(8,128)(2,1)} %constant_dynamic-update-slice_fusion, f32[2048,128]{1,0:T(8,128)S(1)} %copy-done.16, f32[128]{0:T(128)S(1)} %mul.148, f32[128]{0:T(128)S(1)} %sub.99, f32[128]{0:T(128)S(1)} %copy-done.37, f32[128]{0:T(128)S(1)} %copy-done.27, f32[128]{0:T(128)S(1)} %copy-done.29, ...), kind=kOutput, calls=%fused_computation.40 | convolution fusion | flops 1211105280 | bytes 12717056 | tf_op jit(solution)/shard_map/dot_general | solution.py:185
  205.6 2.5 fusion.21
  208.0 1.6 pad_maximum_fusion
  209.8 59.6 %reduce-scatter.2.cloned.1.call-done = f32[16,2,9,128]{3,0,2,1:T(8,128)} async-done(((f32[256,2,9,128]{3,0,2,1:T(8,128)}), f32[16,2,9,128]{3,0,2,1:T(8,128)}) %reduce-scatter.2.cloned.1.call-update) | async-done | bytes 147472 | tf_op jit(solution)/shard_map/reduce_scatter | solution.py:190
  269.4 5.8 %all-reduce.4 = (f32[]{:T(128)}, f32[12,128]{1,0:T(8,128)}) all-reduce(f32[]{:T(128)} %get-tuple-element.22, f32[12,128]{1,0:T(8,128)S(1)} %get-tuple-element.23), channel_id=1, replica_groups=mesh['slide'=2,'tile'=16] {'slide'}, use_global_device_ids=true, to_apply=%region_17.18 | all-reduce | flops 1537 | bytes 12296 | tf_op jit(solution)/shard_map/psum | solution.py:176
  276.5 15.9 %all-reduce.7.cloned.1.call-done = f32[16,2,9,128]{3,0,2,1:T(8,128)} async-done(((f32[16,2,9,128]{3,0,2,1:T(8,128)}), f32[16,2,9,128]{3,0,2,1:T(8,128)}) %all-reduce.7.cloned.1.call-update) | async-done | bytes 147472 | tf_op jit(solution)/shard_map/psum | solution.py:189
  292.4 1.6 copy.16
  (173 shorter events, 31.2 us)
Async XLA Ops:
  7.2 71.3 %copy-start = (bf16[8,128]{1,0:T(8,128)(2,1)S(1)}, bf16[8,128]{1,0:T(8,128)(2,1)}, u32[]{:S(2)}) copy-start(bf16[8,128]{1,0:T(8,128)(2,1)} %param.19) | copy-start | bytes 6148
  7.2 262.2 %reduce-scatter.2.cloned.1.call-start = ((), (), s32[]{:S(2)}) async-start(), calls=%async_computation.1 | async-start | bytes 2506752 | tf_op jit(solution)/shard_map/reduce_scatter | solution.py:190
  8.1 12.6 %collective-permute-start.2 = (bf16[1,128,256]{2,1,0:T(8,128)(2,1)S(1)}, bf16[1,128,256]{2,1,0:T(8,128)(2,1)S(1)}, u32[]{:S(2)}, u32[]{:S(2)}) collective-permute-start(bf16[1,128,256]{2,1,0:T(8,128)(2,1)S(1)} %get-tuple-element.55), channel_id=1, source_target_pairs={{0,1},{1,2},{2,3},{3,4},{4,5},{5,6},{6,7},{7,8},{8,9},{9,10},{10,1... | collective-permute-start | bytes 196616 | tf_op jit(solution)/shard_map/ppermute | solution.py:18
  10.5 10.2 %collective-permute-start.3 = (bf16[1,128,256]{2,1,0:T(8,128)(2,1)S(1)}, bf16[1,128,256]{2,1,0:T(8,128)(2,1)S(1)}, u32[]{:S(2)}, u32[]{:S(2)}) collective-permute-start(bf16[1,128,256]{2,1,0:T(8,128)(2,1)S(1)} %get-tuple-element.56), channel_id=1, source_target_pairs={{1,0},{2,1},{3,2},{4,3},{5,4},{6,5},{7,6},{8,7},{9,8},{10,9},{11,1... | collective-permute-start | bytes 196616 | tf_op jit(solution)/shard_map/ppermute | solution.py:20
  12.8 9.9 %copy-start.20 = (bf16[256,9,128]{2,0,1:T(8,128)(2,1)S(1)}, bf16[256,9,128]{2,0,1:T(8,128)(2,1)}, u32[]{:S(2)}) copy-start(bf16[256,9,128]{2,0,1:T(8,128)(2,1)} %param.14) | copy-start | bytes 1769476
  12.8 19.7 %collective-permute-start = (bf16[1,256,256]{2,1,0:T(8,128)(2,1)S(1)}, bf16[1,256,256]{2,1,0:T(8,128)(2,1)S(1)}, u32[]{:S(2)}, u32[]{:S(2)}) collective-permute-start(bf16[1,256,256]{2,1,0:T(8,128)(2,1)S(1)} %get-tuple-element.45), channel_id=1, source_target_pairs={{0,1},{1,2},{2,3},{3,4},{4,5},{5,6},{6,7},{7,8},{8,9},{9,10},{10,1... | collective-permute-start | bytes 393224 | tf_op jit(solution)/shard_map/ppermute | solution.py:18
  18.1 14.4 %collective-permute-start.1 = (bf16[1,256,256]{2,1,0:T(8,128)(2,1)S(1)}, bf16[1,256,256]{2,1,0:T(8,128)(2,1)S(1)}, u32[]{:S(2)}, u32[]{:S(2)}) collective-permute-start(bf16[1,256,256]{2,1,0:T(8,128)(2,1)S(1)} %get-tuple-element.46), channel_id=1, source_target_pairs={{1,0},{2,1},{3,2},{4,3},{5,4},{6,5},{7,6},{8,7},{9,8},{10,9},{11,1... | collective-permute-start | bytes 393224 | tf_op jit(solution)/shard_map/ppermute | solution.py:20
  27.2 5.9 %copy-start.1 = (bf16[1,8,256,256]{3,2,1,0:T(8,128)(2,1)S(1)}, bf16[1,8,256,256]{3,2,1,0:T(8,128)(2,1)}, u32[]{:S(2)}) copy-start(bf16[1,8,256,256]{3,2,1,0:T(8,128)(2,1)} %param.11) | copy-start | bytes 3145732
  34.2 2.4 copy-start.2
  35.7 2.8 copy-start.8
  38.4 37.7 %copy-start.25 = (f32[128]{0:T(128)S(1)}, f32[128]{0:T(128)}, u32[]{:S(2)}) copy-start(f32[128]{0:T(128)} %param.17) | copy-start | bytes 1540
  38.4 37.7 %copy-start.32 = (f32[128]{0:T(128)S(1)}, f32[128]{0:T(128)}, u32[]{:S(2)}) copy-start(f32[128]{0:T(128)} %param.18) | copy-start | bytes 1540
  40.0 36.7 %copy-start.34 = (f32[128]{0:T(128)S(1)}, f32[128]{0:T(128)}, u32[]{:S(2)}) copy-start(f32[128]{0:T(128)} %param.16) | copy-start | bytes 1540
  40.0 36.7 %copy-start.36 = (f32[128]{0:T(128)S(1)}, f32[128]{0:T(128)}, u32[]{:S(2)}) copy-start(f32[128]{0:T(128)} %param.15) | copy-start | bytes 1540
  76.3 2.5 copy-start.24
  76.3 40.2 %copy-start.23 = (f32[2048]{0:T(1024)S(1)}, f32[2048]{0:T(1024)}, u32[]{:S(2)}) copy-start(f32[2048]{0:T(1024)} %compare_convert_fusion) | copy-start | bytes 24580
  116.4 5.4 %copy-start.12 = (bf16[8,256,256]{2,1,0:T(8,128)(2,1)S(1)}, bf16[8,256,256]{2,1,0:T(8,128)(2,1)}, u32[]{:S(2)}) copy-start(bf16[8,256,256]{2,1,0:T(8,128)(2,1)} %copy-done.11) | copy-start | bytes 3145732
  121.8 4.3 %copy-start.33 = (f32[128]{0:T(128)S(1)}, f32[128]{0:T(128)}, u32[]{:S(2)}) copy-start(f32[128]{0:T(128)} %param.18) | copy-start | bytes 1540
  189.6 2.5 copy-start.5
  189.6 3.6 %copy-start.3 = (bf16[8,256,256]{2,1,0:T(8,128)(2,1)S(1)}, bf16[8,256,256]{2,1,0:T(8,128)(2,1)}, u32[]{:S(2)}) copy-start(bf16[8,256,256]{2,1,0:T(8,128)(2,1)} %copy-done.2) | copy-start | bytes 3145732
  196.5 2.4 copy-start.7
  197.8 2.4 copy-start.27
  200.1 5.4 %copy-start.17 = (f32[512,128]{1,0:T(8,128)S(1)}, f32[512,128]{1,0:T(8,128)}, u32[]{:S(2)}) copy-start(f32[512,128]{1,0:T(8,128)} %get-tuple-element.34) | copy-start | bytes 786436
  209.7 82.7 %all-reduce.7.cloned.1.call-start = ((), (), s32[]{:S(2)}) async-start(), calls=%async_computation.2 | async-start | bytes 294912 | tf_op jit(solution)/shard_map/psum | solution.py:189
  (21 other events, 35.6 us)
Sparse Core Ops, SparseCore 0:
  209.8 59.5 reduce-scatter.1
  271.6 20.6 all-reduce.6
